TPU v7x, 32 devices: a whole 2x2x4 slice. The times are simulated.
32 devices in a mesh: section: 2 (over y), expert: 16 (over z, x, core).
Axes of the slice: x: 2, y: 2, z: 4, core: 2. Of those that a mesh axis runs over, the one named last changes fastest.
Arguments:
- x_in: bfloat16 [4, 64, 7168], P(None, 'expert'), may hold values from -6 to 6
- gains: bfloat16 [2, 7168], P('section'), may hold values from 0.25 to 1.75
- router: bfloat16 [2, 7168, 4], P('section'), may hold values from -0.0625 to 0.0625
- w_gate: bfloat16 [2, 16, 2, 7168, 256], P('section', 'expert'), may hold values from -0.0625 to 0.0625
- w_up: bfloat16 [2, 16, 2, 7168, 256], P('section', 'expert'), may hold values from -0.0625 to 0.0625
- w_down: bfloat16 [2, 16, 2, 256, 7168], P('section', 'expert'), may hold values from -0.125 to 0.125
- route_ids: int32 [2, 4, 64, 2], P('section', None, 'expert'), may hold values from 0 to 3, all different within a row; in each aligned block of 4 rows (0 to 3, 4 to 7, ..., all dimensions but the last counted through in order) at most 2 rows name the same one
- stopped: int32 [4, 64], P(None, 'expert'), may hold values 0 or 1
Outputs:
- layer_out: bfloat16 [2, 4, 64, 7168], P('section', None, 'expert')
Inputs may be any that keep to these rules, and one draw needn't show every extreme that they name: `route_ids`: each row names 2 different experts. Within one layer and micro-batch, the rows of one device (aligned blocks of 4 rows) name one expert at most 2 times.
All inputs are finite; a program needn't handle non-finite values. No bound on the sum of `stopped` on one device may be relied on, other than what follows from the above.
Results may differ from a plain program's by a relative error of at most 0.019.
Values may be sent and summed in bfloat16 or wider, within the bound.
A program may use at most 128 MiB of HBM per device.

v0:
```python
import jax
import jax.numpy as jnp
from jax import lax
from jax.sharding import PartitionSpec as P

SHARDS = 8


def shifted(block, axis, distance):
    devices = range(lax.axis_size(axis))
    route = [(i - distance, i) for i in devices if i - distance in devices]
    return lax.ppermute(block, axis, route)


def slot_hits(chosen, live, experts, slots):
    rows = chosen.shape[0]
    picks = chosen.shape[1]
    flat_ids = chosen.reshape(-1)
    flat_live = jnp.repeat(live, picks)
    onehot = (
        (flat_ids[:, None] == jnp.arange(experts, dtype=jnp.int32)[None, :])
        & (flat_live[:, None] > 0)
    ).astype(jnp.int32)
    place = jnp.cumsum(onehot, axis=0) - onehot
    hits = onehot[:, :, None] * (
        place[:, :, None] == jnp.arange(slots, dtype=jnp.int32)[None, None, :]
    ).astype(jnp.int32)
    return hits.reshape(rows, picks, experts * slots).astype(jnp.float32)


def expert_work(inputs, gate_w, up_w, down_w):
    gate_val = jnp.einsum("slcd,ldh->slch", inputs, gate_w, preferred_element_type=jnp.float32)
    up_val = jnp.einsum("slcd,ldh->slch", inputs, up_w, preferred_element_type=jnp.float32)
    hid = (jax.nn.silu(gate_val) * up_val).astype(jnp.bfloat16)
    return jnp.einsum("slch,lhd->slcd", hid, down_w, preferred_element_type=jnp.float32).astype(
        jnp.bfloat16
    )


def moe_layer(hidden, gain, router_s, gate_w, up_w, down_w, chosen, live):
    rows, width = hidden.shape
    experts = router_s.shape[1]
    picks = chosen.shape[1]
    local = gate_w.shape[0]
    devices = lax.axis_size("expert")
    slots = max(2, rows * picks // experts)
    widened = hidden.astype(jnp.float32)
    mean_sq = jnp.mean(widened * widened, axis=-1, keepdims=True)
    normed = (widened * lax.rsqrt(mean_sq + 1e-06) * gain.astype(jnp.float32)).astype(jnp.bfloat16)
    score = jax.nn.sigmoid(jnp.dot(normed, router_s, preferred_element_type=jnp.float32))
    picked = jnp.take_along_axis(score, chosen, axis=1)
    gates = 2.5 * picked / jnp.sum(picked, axis=1, keepdims=True)
    hits = slot_hits(chosen, live, experts, slots)
    mixing = jnp.sum(hits * gates[:, :, None], axis=1)
    scatter_rows = jnp.transpose(jnp.sum(hits, axis=1)).astype(jnp.bfloat16)
    buffer = jnp.dot(scatter_rows, normed, preferred_element_type=jnp.float32).astype(jnp.bfloat16)
    buffer = buffer.reshape(experts // local, 1, local, slots, width)
    sending = jnp.broadcast_to(buffer, (experts // local, SHARDS, local, slots, width)).reshape(
        devices, local, slots, width
    )
    part = expert_work(
        lax.all_to_all(sending, "expert", split_axis=0, concat_axis=0, tiled=True),
        gate_w,
        up_w,
        down_w,
    )
    returned = lax.all_to_all(part, "expert", split_axis=0, concat_axis=0, tiled=True)
    totals = returned.reshape(experts // local, SHARDS, local, slots, width).astype(jnp.float32)
    totals = jnp.sum(totals, axis=1).reshape(experts * slots, width)
    combined = jnp.dot(
        mixing, totals, precision=lax.Precision.HIGHEST, preferred_element_type=jnp.float32
    )
    return (widened + combined).astype(jnp.bfloat16)


def shards(x_in, gains, router, w_gate, w_up, w_down, route_ids, stopped):
    batches, rows, width = x_in.shape
    sections = lax.axis_size("section")
    section = lax.axis_index("section")
    results = jnp.zeros((batches, rows, width), jnp.bfloat16)
    previous = jnp.zeros((rows, width), jnp.bfloat16)
    for turn in range(batches + sections - 1):
        incoming = shifted(previous, "section", 1)
        current = jnp.where(section == 0, x_in[min(turn, batches - 1)], incoming)
        batch = turn - section
        valid = (batch >= 0) & (batch < batches)
        clipped = jnp.clip(batch, 0, batches - 1)
        stop_row = lax.dynamic_index_in_dim(stopped, clipped, 0, keepdims=False)
        live = (1 - stop_row) * valid.astype(jnp.int32)
        chosen = lax.dynamic_index_in_dim(route_ids[0], clipped, 0, keepdims=False)
        fresh = moe_layer(
            current, gains[0], router[0], w_gate[0, 0], w_up[0, 0], w_down[0, 0], chosen, live
        )
        kept = lax.dynamic_index_in_dim(results, clipped, 0, keepdims=False)
        results = lax.dynamic_update_index_in_dim(
            results, jnp.where(valid, fresh, kept), clipped, 0
        )
        previous = fresh
    return results[None]


def solution(mesh):
    in_specs = (
        P(None, "expert", None),
        P("section", None),
        P("section", None, None),
        P("section", "expert", None, None, None),
        P("section", "expert", None, None, None),
        P("section", "expert", None, None, None),
        P("section", None, "expert", None),
        P(None, "expert"),
    )
    out_specs = P("section", None, "expert", None)
    return jax.shard_map(shards, mesh=mesh, in_specs=in_specs, out_specs=out_specs, check_vma=False)
```

profile of v0, /device:TPU:4, one launch (start us, length us, event | category | flops | bytes accessed | tf_op | source)
XLA Modules:
  0.0 389.0 jit_solution(9595486666969352366)
XLA Ops:
  0.0 1.3 collective-permute-start
  1.3 0.9 compare_bitcast_fusion
  2.4 0.8 bitcast_or_fusion
  3.9 0.8 mul.336
  4.9 1.2 collective-permute-done
  6.1 1.0 fusion.138
  7.4 0.7 gather_fusion
  8.7 0.5 broadcast_in_dim.56
  9.2 28.1 %all_to_all.50 = bf16[16,2,2,7168]{3,2,1,0:T(2,128)(2,1)S(1)} all-to-all(bf16[16,2,2,7168]{3,2,1,0:T(2,128)(2,1)S(1)} %bitcast.308), channel_id=1, replica_groups=mesh['section'=2,'expert'=16] {'expert'}, dimensions={0} | all-to-all | bytes 1835008 | tf_op jit(solution)/shard_map/all_to_all | solution.py:62
  37.3 4.4 %fusion.38 = f32[16,2,2,256]{3,0,2,1:T(8,128)S(1)} fusion(bf16[1,1,2,7168,256]{4,3,2,1,0:T(8,128)(2,1)} %param.13, bf16[16,2,2,7168]{3,2,1,0:T(2,128)(2,1)S(1)} %all_to_all.50), kind=kOutput, calls=%fused_computation.63 | convolution fusion | flops 234881024 | bytes 8323072 | tf_op jit(solution)/shard_map/slcd,ldh->slch/dot_general | solution.py:32
  41.8 7.9 %fusion = bf16[16,2,2,7168]{3,0,2,1:T(8,128)(2,1)S(1)} fusion(bf16[1,1,2,256,7168]{4,3,2,1,0:T(8,128)(2,1)} %param.15, bf16[1,1,2,7168,256]{4,3,2,1,0:T(8,128)(2,1)} %param.14, bf16[16,2,2,7168]{3,2,1,0:T(2,128)(2,1)S(1)} %all_to_all.50, f32[16,2,2,256]{3,0,2,1:T(8,128)S(1)} %fusion.38), kind=kOutput, calls=%fused_computation.10 | convolution fusion | flops 470319104 | bytes 16580608 | tf_op jit(solution)/shard_map/slch,lhd->slcd/dot_general | solution.py:35
  49.7 1.9 copy.105
  51.6 4.5 %all-to-all-start.1 = ((bf16[16,2,2,7168]{3,2,1,0:T(2,128)(2,1)}), bf16[16,2,2,7168]{3,2,1,0:T(2,128)(2,1)S(1)}, u32[]{:S(2)}, u32[]{:S(2)}) async-start(bf16[16,2,2,7168]{3,2,1,0:T(2,128)(2,1)} %copy.105), calls=%async_computation.1 | async-start | bytes 1835008 | tf_op jit(solution)/shard_map/all_to_all | solution.py:67
  56.5 20.3 %all-to-all-done.1 = bf16[16,2,2,7168]{3,2,1,0:T(2,128)(2,1)S(1)} async-done(((bf16[16,2,2,7168]{3,2,1,0:T(2,128)(2,1)}), bf16[16,2,2,7168]{3,2,1,0:T(2,128)(2,1)S(1)}, u32[]{:S(2)}, u32[]{:S(2)}) %all-to-all-start.1) | async-done | bytes 917536 | tf_op jit(solution)/shard_map/all_to_all | solution.py:67
  76.9 0.8 convert_reduce_fusion.4
  78.3 1.3 collective-permute-start.1
  80.2 4.4 %collective-permute-done.1 = bf16[4,7168]{1,0:T(4,128)(2,1)S(1)} collective-permute-done((bf16[4,7168]{1,0:T(4,128)(2,1)S(1)}, bf16[4,7168]{1,0:T(4,128)(2,1)S(1)}, u32[]{:S(2)}, u32[]{:S(2)}) %collective-permute-start.1) | collective-permute-done | bytes 57376 | tf_op jit(solution)/shard_map/ppermute | solution.py:12
  85.0 0.7 gather_fusion.1
  86.4 0.5 broadcast_in_dim.60
  86.8 28.1 %all_to_all.51 = bf16[16,2,2,7168]{3,2,1,0:T(2,128)(2,1)S(1)} all-to-all(bf16[16,2,2,7168]{3,2,1,0:T(2,128)(2,1)S(1)} %bitcast.309), channel_id=1, replica_groups=mesh['section'=2,'expert'=16] {'expert'}, dimensions={0} | all-to-all | bytes 1835008 | tf_op jit(solution)/shard_map/all_to_all | solution.py:62
  115.0 4.4 %fusion.41 = f32[16,2,2,256]{3,0,2,1:T(8,128)S(1)} fusion(bf16[1,1,2,7168,256]{4,3,2,1,0:T(8,128)(2,1)} %param.13, bf16[16,2,2,7168]{3,2,1,0:T(2,128)(2,1)S(1)} %all_to_all.51), kind=kOutput, calls=%fused_computation.64 | convolution fusion | flops 234881024 | bytes 8323072 | tf_op jit(solution)/shard_map/slcd,ldh->slch/dot_general | solution.py:32
  119.4 7.9 %fusion.1 = bf16[16,2,2,7168]{3,0,2,1:T(8,128)(2,1)S(1)} fusion(bf16[1,1,2,256,7168]{4,3,2,1,0:T(8,128)(2,1)} %param.15, bf16[1,1,2,7168,256]{4,3,2,1,0:T(8,128)(2,1)} %param.14, bf16[16,2,2,7168]{3,2,1,0:T(2,128)(2,1)S(1)} %all_to_all.51, f32[16,2,2,256]{3,0,2,1:T(8,128)S(1)} %fusion.41), kind=kOutput, calls=%fused_computation.11 | convolution fusion | flops 470319104 | bytes 16580608 | tf_op jit(solution)/shard_map/slch,lhd->slcd/dot_general | solution.py:35
  127.3 1.9 copy.114
  129.2 4.5 %all-to-all-start.3 = ((bf16[16,2,2,7168]{3,2,1,0:T(2,128)(2,1)}), bf16[16,2,2,7168]{3,2,1,0:T(2,128)(2,1)S(1)}, u32[]{:S(2)}, u32[]{:S(2)}) async-start(bf16[16,2,2,7168]{3,2,1,0:T(2,128)(2,1)} %copy.114), calls=%async_computation.3 | async-start | bytes 1835008 | tf_op jit(solution)/shard_map/all_to_all | solution.py:67
  134.2 20.3 %all-to-all-done.3 = bf16[16,2,2,7168]{3,2,1,0:T(2,128)(2,1)S(1)} async-done(((bf16[16,2,2,7168]{3,2,1,0:T(2,128)(2,1)}), bf16[16,2,2,7168]{3,2,1,0:T(2,128)(2,1)S(1)}, u32[]{:S(2)}, u32[]{:S(2)}) %all-to-all-start.3) | async-done | bytes 917536 | tf_op jit(solution)/shard_map/all_to_all | solution.py:67
  154.5 0.8 convert_reduce_fusion.3
  155.4 0.4 bitcast_dynamic-update-slice_fusion.2
  155.8 1.3 collective-permute-start.2
  157.7 4.4 %collective-permute-done.2 = bf16[4,7168]{1,0:T(4,128)(2,1)S(1)} collective-permute-done((bf16[4,7168]{1,0:T(4,128)(2,1)S(1)}, bf16[4,7168]{1,0:T(4,128)(2,1)S(1)}, u32[]{:S(2)}, u32[]{:S(2)}) %collective-permute-start.2) | collective-permute-done | bytes 57376 | tf_op jit(solution)/shard_map/ppermute | solution.py:12
  162.5 0.7 gather_fusion.2
  163.9 0.5 broadcast_in_dim.64
  164.4 28.2 %all_to_all.52 = bf16[16,2,2,7168]{3,2,1,0:T(2,128)(2,1)S(1)} all-to-all(bf16[16,2,2,7168]{3,2,1,0:T(2,128)(2,1)S(1)} %bitcast.310), channel_id=1, replica_groups=mesh['section'=2,'expert'=16] {'expert'}, dimensions={0} | all-to-all | bytes 1835008 | tf_op jit(solution)/shard_map/all_to_all | solution.py:62
  192.5 4.4 %fusion.44 = f32[16,2,2,256]{3,0,2,1:T(8,128)S(1)} fusion(bf16[1,1,2,7168,256]{4,3,2,1,0:T(8,128)(2,1)} %param.13, bf16[16,2,2,7168]{3,2,1,0:T(2,128)(2,1)S(1)} %all_to_all.52), kind=kOutput, calls=%fused_computation.65 | convolution fusion | flops 234881024 | bytes 8323072 | tf_op jit(solution)/shard_map/slcd,ldh->slch/dot_general | solution.py:32
  196.9 7.9 %fusion.2 = bf16[16,2,2,7168]{3,0,2,1:T(8,128)(2,1)S(1)} fusion(bf16[1,1,2,256,7168]{4,3,2,1,0:T(8,128)(2,1)} %param.15, bf16[1,1,2,7168,256]{4,3,2,1,0:T(8,128)(2,1)} %param.14, bf16[16,2,2,7168]{3,2,1,0:T(2,128)(2,1)S(1)} %all_to_all.52, f32[16,2,2,256]{3,0,2,1:T(8,128)S(1)} %fusion.44), kind=kOutput, calls=%fused_computation.12 | convolution fusion | flops 470319104 | bytes 16580608 | tf_op jit(solution)/shard_map/slch,lhd->slcd/dot_general | solution.py:35
  204.8 1.9 copy.123
  206.7 4.5 %all-to-all-start.5 = ((bf16[16,2,2,7168]{3,2,1,0:T(2,128)(2,1)}), bf16[16,2,2,7168]{3,2,1,0:T(2,128)(2,1)S(1)}, u32[]{:S(2)}, u32[]{:S(2)}) async-start(bf16[16,2,2,7168]{3,2,1,0:T(2,128)(2,1)} %copy.123), calls=%async_computation.5 | async-start | bytes 1835008 | tf_op jit(solution)/shard_map/all_to_all | solution.py:67
  211.7 20.3 %all-to-all-done.5 = bf16[16,2,2,7168]{3,2,1,0:T(2,128)(2,1)S(1)} async-done(((bf16[16,2,2,7168]{3,2,1,0:T(2,128)(2,1)}), bf16[16,2,2,7168]{3,2,1,0:T(2,128)(2,1)S(1)}, u32[]{:S(2)}, u32[]{:S(2)}) %all-to-all-start.5) | async-done | bytes 917536 | tf_op jit(solution)/shard_map/all_to_all | solution.py:67
  232.0 0.8 convert_reduce_fusion.2
  233.0 0.4 bitcast_dynamic-update-slice_fusion.1
  233.3 1.3 collective-permute-start.3
  235.2 4.4 %collective-permute-done.3 = bf16[4,7168]{1,0:T(4,128)(2,1)S(1)} collective-permute-done((bf16[4,7168]{1,0:T(4,128)(2,1)S(1)}, bf16[4,7168]{1,0:T(4,128)(2,1)S(1)}, u32[]{:S(2)}, u32[]{:S(2)}) %collective-permute-start.3) | collective-permute-done | bytes 57376 | tf_op jit(solution)/shard_map/ppermute | solution.py:12
  240.0 0.7 gather_fusion.3
  241.4 0.5 broadcast_in_dim.131
  241.9 28.1 %all_to_all.53 = bf16[16,2,2,7168]{3,2,1,0:T(2,128)(2,1)S(1)} all-to-all(bf16[16,2,2,7168]{3,2,1,0:T(2,128)(2,1)S(1)} %bitcast.311), channel_id=1, replica_groups=mesh['section'=2,'expert'=16] {'expert'}, dimensions={0} | all-to-all | bytes 1835008 | tf_op jit(solution)/shard_map/all_to_all | solution.py:62
  270.1 4.4 %fusion.47 = f32[16,2,2,256]{3,0,2,1:T(8,128)S(1)} fusion(bf16[1,1,2,7168,256]{4,3,2,1,0:T(8,128)(2,1)} %param.13, bf16[16,2,2,7168]{3,2,1,0:T(2,128)(2,1)S(1)} %all_to_all.53), kind=kOutput, calls=%fused_computation.66 | convolution fusion | flops 234881024 | bytes 8323072 | tf_op jit(solution)/shard_map/slcd,ldh->slch/dot_general | solution.py:32
  274.5 7.9 %fusion.3 = bf16[16,2,2,7168]{3,0,2,1:T(8,128)(2,1)S(1)} fusion(bf16[1,1,2,256,7168]{4,3,2,1,0:T(8,128)(2,1)} %param.15, bf16[1,1,2,7168,256]{4,3,2,1,0:T(8,128)(2,1)} %param.14, bf16[16,2,2,7168]{3,2,1,0:T(2,128)(2,1)S(1)} %all_to_all.53, f32[16,2,2,256]{3,0,2,1:T(8,128)S(1)} %fusion.47), kind=kOutput, calls=%fused_computation.13 | convolution fusion | flops 470319104 | bytes 16580608 | tf_op jit(solution)/shard_map/slch,lhd->slcd/dot_general | solution.py:35
  282.3 1.9 copy.132
  284.2 4.5 %all-to-all-start.7 = ((bf16[16,2,2,7168]{3,2,1,0:T(2,128)(2,1)}), bf16[16,2,2,7168]{3,2,1,0:T(2,128)(2,1)S(1)}, u32[]{:S(2)}, u32[]{:S(2)}) async-start(bf16[16,2,2,7168]{3,2,1,0:T(2,128)(2,1)} %copy.132), calls=%async_computation.7 | async-start | bytes 1835008 | tf_op jit(solution)/shard_map/all_to_all | solution.py:67
  289.2 20.3 %all-to-all-done.7 = bf16[16,2,2,7168]{3,2,1,0:T(2,128)(2,1)S(1)} async-done(((bf16[16,2,2,7168]{3,2,1,0:T(2,128)(2,1)}), bf16[16,2,2,7168]{3,2,1,0:T(2,128)(2,1)S(1)}, u32[]{:S(2)}, u32[]{:S(2)}) %all-to-all-start.7) | async-done | bytes 917536 | tf_op jit(solution)/shard_map/all_to_all | solution.py:67
  309.5 0.8 convert_reduce_fusion.1
  310.5 0.4 bitcast_dynamic-update-slice_fusion
  310.9 1.3 collective-permute-start.4
  312.8 4.4 %collective-permute-done.4 = bf16[4,7168]{1,0:T(4,128)(2,1)S(1)} collective-permute-done((bf16[4,7168]{1,0:T(4,128)(2,1)S(1)}, bf16[4,7168]{1,0:T(4,128)(2,1)S(1)}, u32[]{:S(2)}, u32[]{:S(2)}) %collective-permute-start.4) | collective-permute-done | bytes 57376 | tf_op jit(solution)/shard_map/ppermute | solution.py:12
  317.6 0.7 gather_fusion.4
  319.0 0.5 broadcast_in_dim.136
  319.4 28.1 %all_to_all.54 = bf16[16,2,2,7168]{3,2,1,0:T(2,128)(2,1)S(1)} all-to-all(bf16[16,2,2,7168]{3,2,1,0:T(2,128)(2,1)S(1)} %bitcast.312), channel_id=1, replica_groups=mesh['section'=2,'expert'=16] {'expert'}, dimensions={0} | all-to-all | bytes 1835008 | tf_op jit(solution)/shard_map/all_to_all | solution.py:62
  347.6 4.4 %fusion.50 = f32[16,2,2,256]{3,0,2,1:T(8,128)S(1)} fusion(bf16[1,1,2,7168,256]{4,3,2,1,0:T(8,128)(2,1)} %param.13, bf16[16,2,2,7168]{3,2,1,0:T(2,128)(2,1)S(1)} %all_to_all.54), kind=kOutput, calls=%fused_computation.67 | convolution fusion | flops 234881024 | bytes 8323072 | tf_op jit(solution)/shard_map/slcd,ldh->slch/dot_general | solution.py:32
  352.0 7.9 %fusion.4 = bf16[16,2,2,7168]{3,0,2,1:T(8,128)(2,1)S(1)} fusion(bf16[1,1,2,256,7168]{4,3,2,1,0:T(8,128)(2,1)} %param.15, bf16[1,1,2,7168,256]{4,3,2,1,0:T(8,128)(2,1)} %param.14, bf16[16,2,2,7168]{3,2,1,0:T(2,128)(2,1)S(1)} %all_to_all.54, f32[16,2,2,256]{3,0,2,1:T(8,128)S(1)} %fusion.50), kind=kOutput, calls=%fused_computation.14 | convolution fusion | flops 470319104 | bytes 16580608 | tf_op jit(solution)/shard_map/slch,lhd->slcd/dot_general | solution.py:35
  359.9 1.9 copy.141
  361.8 4.5 %all-to-all-start.9 = ((bf16[16,2,2,7168]{3,2,1,0:T(2,128)(2,1)}), bf16[16,2,2,7168]{3,2,1,0:T(2,128)(2,1)S(1)}, u32[]{:S(2)}, u32[]{:S(2)}) async-start(bf16[16,2,2,7168]{3,2,1,0:T(2,128)(2,1)} %copy.141), calls=%async_computation.9 | async-start | bytes 1835008 | tf_op jit(solution)/shard_map/all_to_all | solution.py:67
  366.3 0.7 copy.181
  367.0 20.1 %all-to-all-done.9 = bf16[16,2,2,7168]{3,2,1,0:T(2,128)(2,1)S(1)} async-done(((bf16[16,2,2,7168]{3,2,1,0:T(2,128)(2,1)}), bf16[16,2,2,7168]{3,2,1,0:T(2,128)(2,1)S(1)}, u32[]{:S(2)}, u32[]{:S(2)}) %all-to-all-start.9) | async-done | bytes 917536 | tf_op jit(solution)/shard_map/all_to_all | solution.py:67
  387.1 0.8 convert_reduce_fusion
  388.0 1.0 fusion.12
  (136 shorter events, 11.9 us)
Async XLA Ops:
  0.0 7.1 %copy-start = (bf16[1,7168,4]{1,2,0:T(4,128)(2,1)S(1)}, bf16[1,7168,4]{1,2,0:T(4,128)(2,1)}, u32[]{:S(2)}) copy-start(bf16[1,7168,4]{1,2,0:T(4,128)(2,1)} %param.12) | copy-start | bytes 172036
  0.0 6.1 %collective-permute-start = (bf16[4,7168]{1,0:T(4,128)(2,1)S(1)}, bf16[4,7168]{1,0:T(4,128)(2,1)S(1)}, u32[]{:S(2)}, u32[]{:S(2)}) collective-permute-start(bf16[4,7168]{1,0:T(4,128)(2,1)S(1)} %broadcast_in_dim.53), channel_id=1, source_target_pairs={{0,16},{1,17},{2,18},{3,19},{4,20},{5,21},{6,22},{7,23},{8,24},{9,... | collective-permute-start | bytes 172040 | tf_op jit(solution)/shard_map/ppermute | solution.py:12
  41.8 42.8 %copy-start.1 = (bf16[4,4,7168]{2,1,0:T(4,128)(2,1)S(1)}, bf16[4,4,7168]{2,1,0:T(4,128)(2,1)}, u32[]{:S(2)}) copy-start(bf16[4,4,7168]{2,1,0:T(4,128)(2,1)} %param.10) | copy-start | bytes 688132
  51.6 25.3 %all-to-all-start.1 = ((bf16[16,2,2,7168]{3,2,1,0:T(2,128)(2,1)}), bf16[16,2,2,7168]{3,2,1,0:T(2,128)(2,1)S(1)}, u32[]{:S(2)}, u32[]{:S(2)}) async-start(bf16[16,2,2,7168]{3,2,1,0:T(2,128)(2,1)} %copy.105), calls=%async_computation.1 | async-start | bytes 1835008 | tf_op jit(solution)/shard_map/all_to_all | solution.py:67
  78.3 6.2 %collective-permute-start.1 = (bf16[4,7168]{1,0:T(4,128)(2,1)S(1)}, bf16[4,7168]{1,0:T(4,128)(2,1)S(1)}, u32[]{:S(2)}, u32[]{:S(2)}) collective-permute-start(bf16[4,7168]{1,0:T(4,128)(2,1)S(1)} %get-tuple-element.60), channel_id=1, source_target_pairs={{0,16},{1,17},{2,18},{3,19},{4,20},{5,21},{6,22},{7,23},{8,24},{9,... | collective-permute-start | bytes 172040 | tf_op jit(solution)/shard_map/ppermute | solution.py:12
  129.2 25.3 %all-to-all-start.3 = ((bf16[16,2,2,7168]{3,2,1,0:T(2,128)(2,1)}), bf16[16,2,2,7168]{3,2,1,0:T(2,128)(2,1)S(1)}, u32[]{:S(2)}, u32[]{:S(2)}) async-start(bf16[16,2,2,7168]{3,2,1,0:T(2,128)(2,1)} %copy.114), calls=%async_computation.3 | async-start | bytes 1835008 | tf_op jit(solution)/shard_map/all_to_all | solution.py:67
  155.8 6.2 %collective-permute-start.2 = (bf16[4,7168]{1,0:T(4,128)(2,1)S(1)}, bf16[4,7168]{1,0:T(4,128)(2,1)S(1)}, u32[]{:S(2)}, u32[]{:S(2)}) collective-permute-start(bf16[4,7168]{1,0:T(4,128)(2,1)S(1)} %get-tuple-element.62), channel_id=1, source_target_pairs={{0,16},{1,17},{2,18},{3,19},{4,20},{5,21},{6,22},{7,23},{8,24},{9,... | collective-permute-start | bytes 172040 | tf_op jit(solution)/shard_map/ppermute | solution.py:12
  206.7 25.3 %all-to-all-start.5 = ((bf16[16,2,2,7168]{3,2,1,0:T(2,128)(2,1)}), bf16[16,2,2,7168]{3,2,1,0:T(2,128)(2,1)S(1)}, u32[]{:S(2)}, u32[]{:S(2)}) async-start(bf16[16,2,2,7168]{3,2,1,0:T(2,128)(2,1)} %copy.123), calls=%async_computation.5 | async-start | bytes 1835008 | tf_op jit(solution)/shard_map/all_to_all | solution.py:67
  233.3 6.2 %collective-permute-start.3 = (bf16[4,7168]{1,0:T(4,128)(2,1)S(1)}, bf16[4,7168]{1,0:T(4,128)(2,1)S(1)}, u32[]{:S(2)}, u32[]{:S(2)}) collective-permute-start(bf16[4,7168]{1,0:T(4,128)(2,1)S(1)} %get-tuple-element.64), channel_id=1, source_target_pairs={{0,16},{1,17},{2,18},{3,19},{4,20},{5,21},{6,22},{7,23},{8,24},{9,... | collective-permute-start | bytes 172040 | tf_op jit(solution)/shard_map/ppermute | solution.py:12
  284.2 25.3 %all-to-all-start.7 = ((bf16[16,2,2,7168]{3,2,1,0:T(2,128)(2,1)}), bf16[16,2,2,7168]{3,2,1,0:T(2,128)(2,1)S(1)}, u32[]{:S(2)}, u32[]{:S(2)}) async-start(bf16[16,2,2,7168]{3,2,1,0:T(2,128)(2,1)} %copy.132), calls=%async_computation.7 | async-start | bytes 1835008 | tf_op jit(solution)/shard_map/all_to_all | solution.py:67
  310.9 6.2 %collective-permute-start.4 = (bf16[4,7168]{1,0:T(4,128)(2,1)S(1)}, bf16[4,7168]{1,0:T(4,128)(2,1)S(1)}, u32[]{:S(2)}, u32[]{:S(2)}) collective-permute-start(bf16[4,7168]{1,0:T(4,128)(2,1)S(1)} %get-tuple-element.66), channel_id=1, source_target_pairs={{0,16},{1,17},{2,18},{3,19},{4,20},{5,21},{6,22},{7,23},{8,24},{9,... | collective-permute-start | bytes 172040 | tf_op jit(solution)/shard_map/ppermute | solution.py:12
  361.8 25.3 %all-to-all-start.9 = ((bf16[16,2,2,7168]{3,2,1,0:T(2,128)(2,1)}), bf16[16,2,2,7168]{3,2,1,0:T(2,128)(2,1)S(1)}, u32[]{:S(2)}, u32[]{:S(2)}) async-start(bf16[16,2,2,7168]{3,2,1,0:T(2,128)(2,1)} %copy.141), calls=%async_computation.9 | async-start | bytes 1835008 | tf_op jit(solution)/shard_map/all_to_all | solution.py:67
where the time goes:
time: 392 us; the launch traced here: 389 us
  blocking collectives  141 us (36%)
  waiting for transfers between devices  120 us (31%)
  matrix products  66.5 us (17%)
  starting transfers between devices  29 us (7%)
  local copies, waits for them, and re-layouts  22.8 us (6%)
  other arithmetic  9.66 us (2%)
    all_to_all x5, blocking collectives, moe_layer(): lax.all_to_all(sending, 'expert', split_axis=0, concat_axis=0, tiled=True)  141 us
    all_to_all x5, waiting for transfers between devices, moe_layer(): lax.all_to_all(part, 'expert', split_axis=0, concat_axis=0, tiled=True)  101 us
    dot_general x5, matrix products, expert_work(): jnp.einsum('slch,lhd->slcd', hid, down_w, preferred_element_type=jnp.floa...  39.4 us
    all_to_all x5, starting transfers between devices, moe_layer(): lax.all_to_all(part, 'expert', split_axis=0, concat_axis=0, tiled=True)  22.5 us
    dot_general x5, matrix products, expert_work(): jnp.einsum('slcd,ldh->slch', inputs, gate_w, preferred_element_type=jnp.f...  22.1 us
    ppermute x5, waiting for transfers between devices, shifted(): return lax.ppermute(block, axis, route)  18.6 us
    convert_element_type x5, local copies, waits for them, and re-layouts, expert_work(): jnp.einsum('slch,lhd->slcd', hid, down_w, preferred_element_type=jnp.floa...  9.46 us
  transfers between devices with their start and end apart: 10, of which 10 were waited for; matrix products, arithmetic and copies ran while one was open for 2% of the time, Pallas kernels for 0%

commit v1 on v0

v1 whole, which is shorter than its diff:
```python
import functools

import jax
import jax.numpy as jnp
from jax import lax
from jax.experimental import pallas as pl
from jax.experimental.pallas import tpu as pltpu
from jax.sharding import PartitionSpec as P

SHARDS = 8
CHUNKS = 4
MESH = pl.DeviceIdType.MESH
F32 = jnp.float32
BF16 = jnp.bfloat16


def relay_kernel(
    x_ref, gain_ref, router_ref, ids_ref, stop_ref, wg_hbm, wu_hbm, wd_hbm, out_ref,
    hbuf, wg, wu, wd, rows_all, gate_all, acc, hid, part, recv_core, send_x, recv_x, send_a, recv_a,
    w_sem, a_ss, a_rs, x_ss, x_rs, ci_ss, ci_rs, cj_ss, cj_rs,
    r1_ss, r1_rs, r2_ss, r2_rs, r3_ss, r3_rs, h_ss, h_rs,
):
    rows, width = x_ref.shape
    experts = router_ref.shape[0]
    outer = rows_all.shape[2]
    local = wg.shape[0]
    hidden = wg.shape[2]
    cols = width // CHUNKS
    total = 4 * outer * rows
    sections = lax.axis_size("section")
    section = lax.axis_index("section")
    me = lax.axis_index("expert")
    a = me // 4
    b = (me // 2) % 2
    core = me % 2
    twin = a * 4 + b * 2 + (1 - core)
    across = a * 4 + (1 - b) * 2 + core

    def column(step):
        return lax.rem(a + step, outer)

    def at_column(step):
        return column(step) * 4 + b * 2 + core

    loads = [
        pltpu.make_async_copy(wg_hbm, wg, w_sem.at[0]),
        pltpu.make_async_copy(wu_hbm, wu, w_sem.at[1]),
        pltpu.make_async_copy(wd_hbm, wd, w_sem.at[2]),
    ]
    for load in loads:
        load.start()

    barrier = pltpu.get_barrier_semaphore()
    for peer in [at_column(step) for step in range(1, outer)] + [twin, across]:
        pl.semaphore_signal(barrier, inc=1, device_id={"expert": peer}, device_id_type=MESH)

    @pl.when(section > 0)
    def _():
        pl.semaphore_signal(
            barrier, inc=1, device_id={"section": section - 1}, device_id_type=MESH
        )

    @pl.when(section < sections - 1)
    def _():
        pl.semaphore_signal(
            barrier, inc=1, device_id={"section": section + 1}, device_id_type=MESH
        )

    neighbours = jnp.minimum(section, 1) + jnp.minimum(sections - 1 - section, 1)
    pl.semaphore_wait(barrier, outer + 1 + neighbours)

    def span(c):
        return pl.ds(c * cols, cols)

    def remote(src, dst, ss, rs, where):
        return pltpu.make_async_remote_copy(
            src_ref=src, dst_ref=dst, send_sem=ss, recv_sem=rs, device_id=where, device_id_type=MESH
        )

    def h_copy(c):
        return remote(
            out_ref.at[:, span(c)], hbuf.at[:, span(c)], h_ss.at[c], h_rs.at[c],
            {"section": lax.rem(section + 1, sections)},
        )

    @pl.when(section == 0)
    def _():
        hbuf[...] = x_ref[...]

    squares = jnp.zeros((rows, 1), F32)
    for c in range(CHUNKS):
        @pl.when(section > 0)
        def _():
            h_copy(c).wait_recv()

        piece = hbuf[:, span(c)].astype(F32)
        squares = squares + jnp.sum(piece * piece, axis=1, keepdims=True)
    inverse = lax.rsqrt(squares / width + 1e-06)

    def gather_refs(c, *index):
        if c == CHUNKS:
            return gate_all.at[index]
        return rows_all.at[index + (slice(None),) * (4 - len(index)) + (span(c),)]

    def a_copy(c, step):
        here = gather_refs(c, core, b, a)
        return remote(
            here, here, a_ss.at[c, step - 1], a_rs.at[c, step - 1], {"expert": at_column(step)}
        )

    def x_copy(c):
        here = gather_refs(c, core, b)
        return remote(here, here, x_ss.at[c], x_rs.at[c], {"expert": across})

    def ci_copy(c):
        here = gather_refs(c, core, b)
        return remote(here, here, ci_ss.at[c], ci_rs.at[c], {"expert": twin})

    def cj_copy(c):
        here = gather_refs(c, core, 1 - b)
        return remote(here, here, cj_ss.at[c], cj_rs.at[c], {"expert": twin})

    logits = [jnp.zeros((rows, 1), F32) for _ in range(experts)]
    for c in range(CHUNKS):
        piece = hbuf[:, span(c)].astype(F32)
        normed = (piece * inverse * gain_ref[:, span(c)].astype(F32)).astype(BF16)
        rows_all[core, b, a, :, span(c)] = normed
        for step in range(1, outer):
            a_copy(c, step).start()
        wide = normed.astype(F32)
        for e in range(experts):
            logits[e] = logits[e] + jnp.sum(
                wide * router_ref[e : e + 1, span(c)].astype(F32), axis=1, keepdims=True
            )

    ids = ids_ref[...]
    live = stop_ref[...] == 0
    scores = [jax.nn.sigmoid(value) for value in logits]
    chosen = [(ids[:, 0:1] == e) | (ids[:, 1:2] == e) for e in range(experts)]
    norm = jnp.zeros((rows, 1), F32)
    for e in range(experts):
        norm = norm + jnp.where(chosen[e], scores[e], 0.0)
    lanes = lax.broadcasted_iota(jnp.int32, (rows, 128), 1)
    gates = jnp.zeros((rows, 128), F32)
    for e in range(experts):
        value = jnp.where(chosen[e] & live, 2.5 * scores[e] / norm, 0.0)
        gates = gates + jnp.where(lanes == e, value, 0.0)
    gate_all[core, b, a] = gates
    for step in range(1, outer):
        a_copy(CHUNKS, step).start()

    order = list(range(CHUNKS)) + [CHUNKS]

    def stage_a(c):
        for step in range(1, outer):
            a_copy(c, step).wait_recv()
        x_copy(c).start()
        ci_copy(c).start()

    def stage_x(c):
        x_copy(c).wait_recv()
        cj_copy(c).start()

    def multiply(c):
        ci_copy(c).wait_recv()
        cj_copy(c).wait_recv()
        if c == CHUNKS:
            return
        if c == 0:
            loads[0].wait()
            loads[1].wait()
        block = rows_all[:, :, :, :, span(c)].reshape(total, cols)
        for k in range(local):
            for i, w in enumerate((wg, wu)):
                product = jnp.dot(block, w[k, span(c), :], preferred_element_type=F32)
                if c == 0:
                    acc[k, i] = product
                else:
                    acc[k, i] = acc[k, i] + product

    count = len(order)
    for t in range(count + 2):
        if t < count:
            stage_a(order[t])
        if 1 <= t < count + 1:
            stage_x(order[t - 1])
        if t >= 2:
            multiply(order[t - 2])

    weights = gate_all[...].reshape(total, 128)
    lanes_all = lax.broadcasted_iota(jnp.int32, (total, 128), 1)
    for k in range(local):
        expert = local * (me // SHARDS) + k
        weight = jnp.sum(jnp.where(lanes_all == expert, weights, 0.0), axis=1, keepdims=True)
        value = acc[k, 0]
        value = value / (1.0 + jnp.exp(-value)) * acc[k, 1]
        hid[:, k * hidden : (k + 1) * hidden] = jnp.where(
            weight != 0.0, value * weight, 0.0
        ).astype(BF16)

    loads[2].wait()

    def r1_copy(c):
        return remote(
            part.at[1 - core, :, :, :, span(c)], recv_core.at[:, :, :, span(c)],
            r1_ss.at[c], r1_rs.at[c], {"expert": twin},
        )

    def r2_copy(c):
        return remote(
            send_x.at[:, :, span(c)], recv_x.at[:, :, span(c)],
            r2_ss.at[c], r2_rs.at[c], {"expert": across},
        )

    def r3_copy(c, step):
        return remote(
            send_a.at[step - 1, :, span(c)], recv_a.at[step - 1, :, span(c)],
            r3_ss.at[c, step - 1], r3_rs.at[c, step - 1], {"expert": at_column(step)},
        )

    tile = 256

    def down(c):
        @pl.loop(0, cols // tile)
        def _(j):
            at = pl.ds(pl.multiple_of(c * cols + j * tile, tile), tile)
            product = jnp.dot(hid[...], wd[:, at], preferred_element_type=F32)
            part[:, :, :, :, at] = product.astype(BF16).reshape(2, 2, outer, rows, tile)

        r1_copy(c).start()

    def add_core(c):
        r1_copy(c).wait_recv()
        for i in range(outer):
            send_x[i, :, span(c)] = (
                part[core, 1 - b, i, :, span(c)].astype(F32)
                + recv_core[1 - b, i, :, span(c)].astype(F32)
            ).astype(BF16)
        r2_copy(c).start()

    def column_sum(c, i):
        return (
            part[core, b, i, :, span(c)].astype(F32)
            + recv_core[b, i, :, span(c)].astype(F32)
            + recv_x[i, :, span(c)].astype(F32)
        )

    def add_x(c):
        r2_copy(c).wait_recv()
        for step in range(1, outer):
            send_a[step - 1, :, span(c)] = column_sum(c, column(step)).astype(BF16)
            r3_copy(c, step).start()

    def finish(c):
        result = column_sum(c, a)
        for step in range(1, outer):
            r3_copy(c, step).wait_recv()
            result = result + recv_a[step - 1, :, span(c)].astype(F32)
        out_ref[:, span(c)] = (hbuf[:, span(c)].astype(F32) + result).astype(BF16)

        @pl.when(section < sections - 1)
        def _():
            h_copy(c).start()

    for t in range(CHUNKS + 3):
        if t < CHUNKS:
            down(t)
        if 1 <= t < CHUNKS + 1:
            add_core(t - 1)
        if 2 <= t < CHUNKS + 2:
            add_x(t - 2)
        if t >= 3:
            finish(t - 3)

    for c in order:
        for step in range(1, outer):
            a_copy(c, step).wait_send()
        x_copy(c).wait_send()
        ci_copy(c).wait_send()
        cj_copy(c).wait_send()
    for c in range(CHUNKS):
        r1_copy(c).wait_send()
        r2_copy(c).wait_send()
        for step in range(1, outer):
            r3_copy(c, step).wait_send()

    @pl.when(section < sections - 1)
    def _():
        for c in range(CHUNKS):
            h_copy(c).wait_send()


def shards(x_in, gains, router, w_gate, w_up, w_down, route_ids, stopped):
    batches, per, width = x_in.shape
    rows = batches * per
    local, _, hidden = w_gate.shape[2:]
    experts = router.shape[2]
    picks = route_ids.shape[3]
    outer = lax.axis_size("expert") // 4
    dma = lambda *shape: pltpu.SemaphoreType.DMA(shape)
    vmem = pl.BlockSpec(memory_space=pltpu.VMEM)
    anywhere = pl.BlockSpec(memory_space=pl.ANY)
    total = 4 * outer * rows
    more = CHUNKS + 1
    result = pl.pallas_call(
        relay_kernel,
        out_shape=jax.ShapeDtypeStruct((rows, width), BF16),
        in_specs=[vmem] * 5 + [anywhere] * 3,
        out_specs=vmem,
        scratch_shapes=[
            pltpu.VMEM((rows, width), BF16),
            pltpu.VMEM((local, width, hidden), BF16),
            pltpu.VMEM((local, width, hidden), BF16),
            pltpu.VMEM((local * hidden, width), BF16),
            pltpu.VMEM((2, 2, outer, rows, width), BF16),
            pltpu.VMEM((2, 2, outer, rows, 128), F32),
            pltpu.VMEM((local, 2, total, hidden), F32),
            pltpu.VMEM((total, local * hidden), BF16),
            pltpu.VMEM((2, 2, outer, rows, width), BF16),
            pltpu.VMEM((2, outer, rows, width), BF16),
            pltpu.VMEM((outer, rows, width), BF16),
            pltpu.VMEM((outer, rows, width), BF16),
            pltpu.VMEM((outer - 1, rows, width), BF16),
            pltpu.VMEM((outer - 1, rows, width), BF16),
            dma(3),
            dma(more, outer - 1), dma(more, outer - 1),
            dma(more), dma(more), dma(more), dma(more), dma(more), dma(more),
            dma(CHUNKS), dma(CHUNKS), dma(CHUNKS), dma(CHUNKS),
            dma(CHUNKS, outer - 1), dma(CHUNKS, outer - 1),
            dma(CHUNKS), dma(CHUNKS),
        ],
        compiler_params=pltpu.CompilerParams(
            collective_id=0, has_side_effects=True, vmem_limit_bytes=66 * 1000 * 1000
        ),
    )(
        x_in.reshape(rows, width),
        gains,
        jnp.transpose(router[0]),
        route_ids.reshape(rows, picks),
        stopped.reshape(rows, 1),
        w_gate[0, 0],
        w_up[0, 0],
        w_down.reshape(local * hidden, width),
    )
    return result.reshape(1, batches, per, width)


def solution(mesh):
    in_specs = (
        P(None, "expert", None),
        P("section", None),
        P("section", None, None),
        P("section", "expert", None, None, None),
        P("section", "expert", None, None, None),
        P("section", "expert", None, None, None),
        P("section", None, "expert", None),
        P(None, "expert"),
    )
    out_specs = P("section", None, "expert", None)
    return jax.shard_map(shards, mesh=mesh, in_specs=in_specs, out_specs=out_specs, check_vma=False)
```

time: 392 us -> 144 us (0.37)
  blocking collectives: 141 us -> 0 us
  Pallas kernels: 0 us -> 138 us
  waiting for transfers between devices: 120 us -> 0 us
  matrix products: 66.5 us -> 0 us
  starting transfers between devices: 29 us -> 0 us
  local copies, waits for them, and re-layouts: 22.8 us -> 6.13 us
  other arithmetic: 9.66 us -> 0 us
    all_to_all x5 -> x0, blocking collectives: 141 us -> none  [moe_layer(): lax.all_to_all(sending, 'expert', split_axis=0, concat_axis=0, tiled=True)]
    pallas_call x0 -> x1, Pallas kernels: none -> 138 us  [shards(): pl.pallas_call(relay_kernel, out_shape=jax.ShapeDtypeStruct((rows, width)...]
    all_to_all x5 -> x0, waiting for transfers between devices: 101 us -> none  [moe_layer(): lax.all_to_all(part, 'expert', split_axis=0, concat_axis=0, tiled=True)]
    dot_general x25 -> x0, matrix products: 66.5 us -> none  [the longest x5 39.4 us: expert_work(): jnp.einsum('slch,lhd->slcd', hid, down_w, preferred_element_type=jnp.floa...]
    all_to_all x5 -> x0, starting transfers between devices: 22.5 us -> none  [moe_layer(): lax.all_to_all(part, 'expert', split_axis=0, concat_axis=0, tiled=True)]
    ppermute x5 -> x0, waiting for transfers between devices: 18.6 us -> none  [shifted(): return lax.ppermute(block, axis, route)]
    convert_element_type x5 -> x0, local copies, waits for them, and re-layouts: 9.46 us -> none  [expert_work(): jnp.einsum('slch,lhd->slcd', hid, down_w, preferred_element_type=jnp.floa...]
    ppermute x5 -> x0, starting transfers between devices: 6.46 us -> none  [shifted(): return lax.ppermute(block, axis, route)]
  transfers between devices with their start and end apart: 10 -> 0, of which waited for: 10 -> 0; matrix products, arithmetic and copies ran while one was open for 2% -> 0% of each run, Pallas kernels for 0% -> 0%
where the time goes in v1:
time: 144 us
  Pallas kernels  138 us (96%)
  local copies, waits for them, and re-layouts  6.13 us (4%)
    pallas_call x1, Pallas kernels, shards(): pl.pallas_call(relay_kernel, out_shape=jax.ShapeDtypeStruct((rows, width)...  138 us

profile of v1, /device:TPU:4, one launch (start us, length us, event | category | flops | bytes accessed | tf_op | source)
XLA Modules:
  0.0 144.2 jit_solution(14468385544680526739)
XLA Ops:
  0.0 1.4 copy.12
  1.4 1.3 reshape.20.stop_ref
  2.7 1.7 %reshape.15.x_ref = bf16[16,7168]{1,0:T(8,128)(2,1)} reshape(bf16[4,4,7168]{2,1,0:T(4,128)(2,1)} %param.8) | data formatting | bytes 458752 | tf_op jit(solution)/shard_map/reshape | solution.py:336
  4.4 138.1 %shard_map.82 = bf16[16,7168]{1,0:T(8,128)(2,1)} custom-call(bf16[16,7168]{1,0:T(8,128)(2,1)} %reshape.15.x_ref, bf16[1,7168]{1,0:T(2,128)(2,1)} %gain_ref.1, bf16[4,7168]{1,0:T(4,128)(2,1)} %bitcast.10, s32[16,2]{1,0:T(8,128)} %bitcast.11, s32[16,1]{1,0:T(8,128)} %reshape.20.stop_ref, bf16[2,7168,256]{2,1,0:T(8,128)(2,1)} %bitcast.7, ...), custom_call_target="tpu_custom_call" | custom-call | tf_op jit(solution)/shard_map/pallas_call | solution.py:305
  142.5 1.7 %reshape.19 = bf16[1,4,4,7168]{3,2,1,0:T(4,128)(2,1)} reshape(bf16[16,7168]{1,0:T(8,128)(2,1)} %shard_map.82) | data formatting | bytes 458752 | tf_op jit(solution)/shard_map/reshape | solution.py:345

commit v2 on v1

v2 whole, which is shorter than its diff:
```python
import functools

import jax
import jax.numpy as jnp
from jax import lax
from jax.experimental import pallas as pl
from jax.experimental.pallas import tpu as pltpu
from jax.sharding import PartitionSpec as P

SHARDS = 8
CHUNKS = 4
PARTS = 2
MESH = pl.DeviceIdType.MESH
F32 = jnp.float32
BF16 = jnp.bfloat16


def relay_kernel(
    x_ref, gain_ref, router_ref, ids_ref, stop_ref, wg_hbm, wu_hbm, wd_hbm, out_ref,
    hbuf, wg, wu, wd, rows_all, gate_all, acc, hid, part, recv_core, send_x, recv_x, send_a, recv_a,
    w_sem, a_ss, a_rs, x_ss, x_rs, ci_ss, ci_rs, cj_ss, cj_rs,
    r1_ss, r1_rs, r2_ss, r2_rs, r3_ss, r3_rs, h_ss, h_rs,
):
    _, rows, width = x_ref.shape
    experts = router_ref.shape[0]
    outer = rows_all.shape[3]
    local = wg.shape[0]
    hidden = wg.shape[2]
    cols = width // CHUNKS
    total = 4 * outer * rows
    sections = lax.axis_size("section")
    section = lax.axis_index("section")
    me = lax.axis_index("expert")
    a = me // 4
    b = (me // 2) % 2
    core = me % 2
    twin = a * 4 + b * 2 + (1 - core)
    across = a * 4 + (1 - b) * 2 + core

    def column(step):
        return lax.rem(a + step, outer)

    def at_column(step):
        return column(step) * 4 + b * 2 + core

    loads = [
        pltpu.make_async_copy(wg_hbm, wg, w_sem.at[0]),
        pltpu.make_async_copy(wu_hbm, wu, w_sem.at[1]),
        pltpu.make_async_copy(wd_hbm, wd, w_sem.at[2]),
    ]
    for load in loads:
        load.start()

    barrier = pltpu.get_barrier_semaphore()
    for peer in [at_column(step) for step in range(1, outer)] + [twin, across]:
        pl.semaphore_signal(barrier, inc=1, device_id={"expert": peer}, device_id_type=MESH)

    @pl.when(section > 0)
    def _():
        pl.semaphore_signal(
            barrier, inc=1, device_id={"section": section - 1}, device_id_type=MESH
        )

    @pl.when(section < sections - 1)
    def _():
        pl.semaphore_signal(
            barrier, inc=1, device_id={"section": section + 1}, device_id_type=MESH
        )

    neighbours = jnp.minimum(section, 1) + jnp.minimum(sections - 1 - section, 1)
    pl.semaphore_wait(barrier, outer + 1 + neighbours)

    def span(c):
        return pl.ds(c * cols, cols)

    def remote(src, dst, ss, rs, where):
        return pltpu.make_async_remote_copy(
            src_ref=src, dst_ref=dst, send_sem=ss, recv_sem=rs, device_id=where, device_id_type=MESH
        )

    def h_copy(p, c):
        return remote(
            out_ref.at[p, :, span(c)], hbuf.at[p, :, span(c)], h_ss.at[p, c], h_rs.at[p, c],
            {"section": lax.rem(section + 1, sections)},
        )

    @pl.when(section == 0)
    def _():
        hbuf[...] = x_ref[...]

    def gather_refs(p, c, *index):
        if c == CHUNKS:
            return gate_all.at[(p,) + index]
        return rows_all.at[(p,) + index + (slice(None),) * (4 - len(index)) + (span(c),)]

    def a_copy(p, c, step):
        here = gather_refs(p, c, core, b, a)
        return remote(
            here, here, a_ss.at[p, c, step - 1], a_rs.at[p, c, step - 1],
            {"expert": at_column(step)},
        )

    def x_copy(p, c):
        here = gather_refs(p, c, core, b)
        return remote(here, here, x_ss.at[p, c], x_rs.at[p, c], {"expert": across})

    def ci_copy(p, c):
        here = gather_refs(p, c, core, b)
        return remote(here, here, ci_ss.at[p, c], ci_rs.at[p, c], {"expert": twin})

    def cj_copy(p, c):
        here = gather_refs(p, c, core, 1 - b)
        return remote(here, here, cj_ss.at[p, c], cj_rs.at[p, c], {"expert": twin})

    def send_rows(p, waits):
        squares = jnp.zeros((rows, 1), F32)
        for c in range(CHUNKS):
            if waits:
                h_copy(p, c).wait_recv()
            piece = hbuf[p, :, span(c)].astype(F32)
            squares = squares + jnp.sum(piece * piece, axis=1, keepdims=True)
        inverse = lax.rsqrt(squares / width + 1e-06)
        logits = [jnp.zeros((rows, 1), F32) for _ in range(experts)]
        for c in range(CHUNKS):
            piece = hbuf[p, :, span(c)].astype(F32)
            normed = (piece * inverse * gain_ref[:, span(c)].astype(F32)).astype(BF16)
            rows_all[p, core, b, a, :, span(c)] = normed
            for step in range(1, outer):
                a_copy(p, c, step).start()
            wide = normed.astype(F32)
            for e in range(experts):
                logits[e] = logits[e] + jnp.sum(
                    wide * router_ref[e : e + 1, span(c)].astype(F32), axis=1, keepdims=True
                )
        ids = ids_ref[p]
        live = stop_ref[p] == 0
        scores = [jax.nn.sigmoid(value) for value in logits]
        chosen = [(ids[:, 0:1] == e) | (ids[:, 1:2] == e) for e in range(experts)]
        norm = jnp.zeros((rows, 1), F32)
        for e in range(experts):
            norm = norm + jnp.where(chosen[e], scores[e], 0.0)
        lanes = lax.broadcasted_iota(jnp.int32, (rows, 128), 1)
        gates = jnp.zeros((rows, 128), F32)
        for e in range(experts):
            value = jnp.where(chosen[e] & live, 2.5 * scores[e] / norm, 0.0)
            gates = gates + jnp.where(lanes == e, value, 0.0)
        gate_all[p, core, b, a] = gates
        for step in range(1, outer):
            a_copy(p, CHUNKS, step).start()

    def stage_a(p, c):
        for step in range(1, outer):
            a_copy(p, c, step).wait_recv()
        x_copy(p, c).start()
        ci_copy(p, c).start()

    def stage_x(p, c):
        x_copy(p, c).wait_recv()
        cj_copy(p, c).start()

    def multiply(p, c):
        ci_copy(p, c).wait_recv()
        cj_copy(p, c).wait_recv()
        if c == CHUNKS:
            return
        if c == 0 and p == 0:
            loads[0].wait()
            loads[1].wait()
        block = rows_all[p, :, :, :, :, span(c)].reshape(total, cols)
        for k in range(local):
            for i, w in enumerate((wg, wu)):
                product = jnp.dot(block, w[k, span(c), :], preferred_element_type=F32)
                if c == 0:
                    acc[k, i] = product
                else:
                    acc[k, i] = acc[k, i] + product

    def activate(p):
        weights = gate_all[p].reshape(total, 128)
        lanes_all = lax.broadcasted_iota(jnp.int32, (total, 128), 1)
        for k in range(local):
            expert = local * (me // SHARDS) + k
            weight = jnp.sum(jnp.where(lanes_all == expert, weights, 0.0), axis=1, keepdims=True)
            value = acc[k, 0]
            value = value / (1.0 + jnp.exp(-value)) * acc[k, 1]
            hid[:, k * hidden : (k + 1) * hidden] = jnp.where(
                weight != 0.0, value * weight, 0.0
            ).astype(BF16)

    def r1_copy(p, c):
        return remote(
            part.at[p, 1 - core, :, :, :, span(c)], recv_core.at[p, :, :, :, span(c)],
            r1_ss.at[p, c], r1_rs.at[p, c], {"expert": twin},
        )

    def r2_copy(p, c):
        return remote(
            send_x.at[p, :, :, span(c)], recv_x.at[p, :, :, span(c)],
            r2_ss.at[p, c], r2_rs.at[p, c], {"expert": across},
        )

    def r3_copy(p, c, step):
        return remote(
            send_a.at[p, step - 1, :, span(c)], recv_a.at[p, step - 1, :, span(c)],
            r3_ss.at[p, c, step - 1], r3_rs.at[p, c, step - 1], {"expert": at_column(step)},
        )

    tile = 256

    def down(p, c):
        if c == 0 and p == 0:
            loads[2].wait()

        @pl.loop(0, cols // tile)
        def _(j):
            at = pl.ds(pl.multiple_of(c * cols + j * tile, tile), tile)
            product = jnp.dot(hid[...], wd[:, at], preferred_element_type=F32)
            part[p, :, :, :, :, at] = product.reshape(2, 2, outer, rows, tile).astype(BF16)

        r1_copy(p, c).start()

    def add_core(p, c):
        r1_copy(p, c).wait_recv()
        for i in range(outer):
            send_x[p, i, :, span(c)] = (
                part[p, core, 1 - b, i, :, span(c)].astype(F32)
                + recv_core[p, 1 - b, i, :, span(c)].astype(F32)
            ).astype(BF16)
        r2_copy(p, c).start()

    def column_sum(p, c, i):
        return (
            part[p, core, b, i, :, span(c)].astype(F32)
            + recv_core[p, b, i, :, span(c)].astype(F32)
            + recv_x[p, i, :, span(c)].astype(F32)
        )

    def add_x(p, c):
        r2_copy(p, c).wait_recv()
        for step in range(1, outer):
            send_a[p, step - 1, :, span(c)] = column_sum(p, c, column(step)).astype(BF16)
            r3_copy(p, c, step).start()

    def finish(p, c):
        result = column_sum(p, c, a)
        for step in range(1, outer):
            r3_copy(p, c, step).wait_recv()
            result = result + recv_a[p, step - 1, :, span(c)].astype(F32)
        out_ref[p, :, span(c)] = (hbuf[p, :, span(c)].astype(F32) + result).astype(BF16)

        @pl.when(section < sections - 1)
        def _():
            h_copy(p, c).start()

    everything = CHUNKS + 1

    @pl.when(section == 0)
    def _():
        for p in range(PARTS):
            send_rows(p, False)

    @pl.when(section > 0)
    def _():
        send_rows(0, True)

    for p in range(PARTS + 1):
        for t in range(CHUNKS + 4):
            if p > 0 and t < CHUNKS:
                down(p - 1, t)
            if p < PARTS and t < everything:
                stage_a(p, t)
            if p > 0 and 1 <= t < CHUNKS + 1:
                add_core(p - 1, t - 1)
            if p < PARTS and 1 <= t < everything + 1:
                stage_x(p, t - 1)
            if p > 0 and 2 <= t < CHUNKS + 2:
                add_x(p - 1, t - 2)
            if p + 1 < PARTS and t == everything:

                @pl.when(section > 0)
                def _():
                    send_rows(p + 1, True)

            if p < PARTS and 2 <= t < everything + 2:
                multiply(p, t - 2)
            if p > 0 and 3 <= t < CHUNKS + 3:
                finish(p - 1, t - 3)
        if p < PARTS:
            activate(p)

    for p in range(PARTS):
        for c in range(everything):
            for step in range(1, outer):
                a_copy(p, c, step).wait_send()
            x_copy(p, c).wait_send()
            ci_copy(p, c).wait_send()
            cj_copy(p, c).wait_send()
        for c in range(CHUNKS):
            r1_copy(p, c).wait_send()
            r2_copy(p, c).wait_send()
            for step in range(1, outer):
                r3_copy(p, c, step).wait_send()

    @pl.when(section < sections - 1)
    def _():
        for p in range(PARTS):
            for c in range(CHUNKS):
                h_copy(p, c).wait_send()


def shards(x_in, gains, router, w_gate, w_up, w_down, route_ids, stopped):
    batches, per, width = x_in.shape
    rows = batches * per // PARTS
    local, _, hidden = w_gate.shape[2:]
    experts = router.shape[2]
    picks = route_ids.shape[3]
    outer = lax.axis_size("expert") // 4
    dma = lambda *shape: pltpu.SemaphoreType.DMA(shape)
    vmem = pl.BlockSpec(memory_space=pltpu.VMEM)
    anywhere = pl.BlockSpec(memory_space=pl.ANY)
    total = 4 * outer * rows
    more = CHUNKS + 1
    result = pl.pallas_call(
        relay_kernel,
        out_shape=jax.ShapeDtypeStruct((PARTS, rows, width), BF16),
        in_specs=[vmem] * 5 + [anywhere] * 3,
        out_specs=vmem,
        scratch_shapes=[
            pltpu.VMEM((PARTS, rows, width), BF16),
            pltpu.VMEM((local, width, hidden), BF16),
            pltpu.VMEM((local, width, hidden), BF16),
            pltpu.VMEM((local * hidden, width), BF16),
            pltpu.VMEM((PARTS, 2, 2, outer, rows, width), BF16),
            pltpu.VMEM((PARTS, 2, 2, outer, rows, 128), F32),
            pltpu.VMEM((local, 2, total, hidden), F32),
            pltpu.VMEM((total, local * hidden), BF16),
            pltpu.VMEM((PARTS, 2, 2, outer, rows, width), BF16),
            pltpu.VMEM((PARTS, 2, outer, rows, width), BF16),
            pltpu.VMEM((PARTS, outer, rows, width), BF16),
            pltpu.VMEM((PARTS, outer, rows, width), BF16),
            pltpu.VMEM((PARTS, outer - 1, rows, width), BF16),
            pltpu.VMEM((PARTS, outer - 1, rows, width), BF16),
            dma(3),
            dma(PARTS, more, outer - 1), dma(PARTS, more, outer - 1),
            dma(PARTS, more), dma(PARTS, more), dma(PARTS, more), dma(PARTS, more), dma(PARTS, more), dma(PARTS, more),
            dma(PARTS, CHUNKS), dma(PARTS, CHUNKS), dma(PARTS, CHUNKS), dma(PARTS, CHUNKS),
            dma(PARTS, CHUNKS, outer - 1), dma(PARTS, CHUNKS, outer - 1),
            dma(PARTS, CHUNKS), dma(PARTS, CHUNKS),
        ],
        compiler_params=pltpu.CompilerParams(
            collective_id=0, has_side_effects=True, vmem_limit_bytes=66 * 1000 * 1000
        ),
    )(
        x_in.reshape(PARTS, rows, width),
        gains,
        jnp.transpose(router[0]),
        route_ids.reshape(PARTS, rows, picks),
        stopped.reshape(PARTS, rows, 1),
        w_gate[0, 0],
        w_up[0, 0],
        w_down.reshape(local * hidden, width),
    )
    return result.reshape(1, batches, per, width)


def solution(mesh):
    in_specs = (
        P(None, "expert", None),
        P("section", None),
        P("section", None, None),
        P("section", "expert", None, None, None),
        P("section", "expert", None, None, None),
        P("section", "expert", None, None, None),
        P("section", None, "expert", None),
        P(None, "expert"),
    )
    out_specs = P("section", None, "expert", None)
    return jax.shard_map(shards, mesh=mesh, in_specs=in_specs, out_specs=out_specs, check_vma=False)
```

time: 144 us -> 137 us (0.951)
  Pallas kernels: 138 us -> 131 us
    pallas_call x1, Pallas kernels: 138 us -> 131 us  [shards(): pl.pallas_call(relay_kernel, out_shape=jax.ShapeDtypeStruct((PARTS, rows,...]
where the time goes in v2:
time: 137 us
  Pallas kernels  131 us (96%)
  local copies, waits for them, and re-layouts  6.13 us (4%)
    pallas_call x1, Pallas kernels, shards(): pl.pallas_call(relay_kernel, out_shape=jax.ShapeDtypeStruct((PARTS, rows,...  131 us

profile of v2, /device:TPU:4, one launch (start us, length us, event | category | flops | bytes accessed | tf_op | source)
XLA Modules:
  0.0 137.2 jit_solution(17192451716551000661)
XLA Ops:
  0.0 1.4 %copy.12 = s32[1,4,4,2]{3,2,1,0:T(4,128)} copy(s32[1,4,4,2]{2,3,1,0:T(2,128)} %param.14) | data formatting | bytes 256 | tf_op jit(solution)/shard_map/reshape | solution.py:357
  1.4 1.3 reshape.20.stop_ref
  2.7 1.7 %reshape.15.x_ref = bf16[2,8,7168]{2,1,0:T(8,128)(2,1)} reshape(bf16[4,4,7168]{2,1,0:T(4,128)(2,1)} %param.8) | data formatting | bytes 458752 | tf_op jit(solution)/shard_map/reshape | solution.py:354
  4.4 131.1 %shard_map.82 = bf16[2,8,7168]{2,1,0:T(8,128)(2,1)} custom-call(bf16[2,8,7168]{2,1,0:T(8,128)(2,1)} %reshape.15.x_ref, bf16[1,7168]{1,0:T(2,128)(2,1)} %gain_ref.1, bf16[4,7168]{1,0:T(4,128)(2,1)} %bitcast.10, s32[2,8,2]{2,1,0:T(8,128)} %bitcast.11, s32[2,8,1]{2,1,0:T(8,128)} %reshape.20.stop_ref, bf16[2,7168,256]{2,1,0:T(8,128)(2,1)} %bitcast.7, ...), custom_call_target="tpu_custom_call" | custom-call | tf_op jit(solution)/shard_map/pallas_call | solution.py:323
  135.5 1.7 %reshape.19 = bf16[1,4,4,7168]{3,2,1,0:T(4,128)(2,1)} reshape(bf16[2,8,7168]{2,1,0:T(8,128)(2,1)} %shard_map.82) | data formatting | bytes 458752 | tf_op jit(solution)/shard_map/reshape | solution.py:363

commit v3 on v2

--- a/solution.py
+++ b/solution.py
@@ -8,8 +8,10 @@
 from jax.sharding import PartitionSpec as P
 
 SHARDS = 8
-CHUNKS = 4
+CHUNKS = 7
 PARTS = 2
+GATHER_LAGS = (2, 3)
+REDUCE_LAGS = (1, 3, 5)
 MESH = pl.DeviceIdType.MESH
 F32 = jnp.float32
 BF16 = jnp.bfloat16
@@ -263,28 +265,32 @@
     def _():
         send_rows(0, True)
 
+    def due(t, lag, count):
+        return lag <= t < lag + count
+
     for p in range(PARTS + 1):
-        for t in range(CHUNKS + 4):
-            if p > 0 and t < CHUNKS:
+        steps = max(everything + GATHER_LAGS[-1], CHUNKS + REDUCE_LAGS[-1])
+        for t in range(steps):
+            if p > 0 and due(t, 0, CHUNKS):
                 down(p - 1, t)
-            if p < PARTS and t < everything:
+            if p < PARTS and due(t, 0, everything):
                 stage_a(p, t)
-            if p > 0 and 1 <= t < CHUNKS + 1:
-                add_core(p - 1, t - 1)
-            if p < PARTS and 1 <= t < everything + 1:
-                stage_x(p, t - 1)
-            if p > 0 and 2 <= t < CHUNKS + 2:
-                add_x(p - 1, t - 2)
+            if p > 0 and due(t, REDUCE_LAGS[0], CHUNKS):
+                add_core(p - 1, t - REDUCE_LAGS[0])
+            if p < PARTS and due(t, GATHER_LAGS[0], everything):
+                stage_x(p, t - GATHER_LAGS[0])
+            if p > 0 and due(t, REDUCE_LAGS[1], CHUNKS):
+                add_x(p - 1, t - REDUCE_LAGS[1])
             if p + 1 < PARTS and t == everything:
 
                 @pl.when(section > 0)
                 def _():
                     send_rows(p + 1, True)
 
-            if p < PARTS and 2 <= t < everything + 2:
-                multiply(p, t - 2)
-            if p > 0 and 3 <= t < CHUNKS + 3:
-                finish(p - 1, t - 3)
+            if p < PARTS and due(t, GATHER_LAGS[1], everything):
+                multiply(p, t - GATHER_LAGS[1])
+            if p > 0 and due(t, REDUCE_LAGS[2], CHUNKS):
+                finish(p - 1, t - REDUCE_LAGS[2])
         if p < PARTS:
             activate(p)
 

time: 137 us -> 133 us (0.971)
  Pallas kernels: 131 us -> 127 us
    pallas_call x1, Pallas kernels: 131 us -> 127 us  [shards(): pl.pallas_call(relay_kernel, out_shape=jax.ShapeDtypeStruct((PARTS, rows,...]
where the time goes in v3:
time: 133 us
  Pallas kernels  127 us (95%)
  local copies, waits for them, and re-layouts  6.13 us (5%)
    pallas_call x1, Pallas kernels, shards(): pl.pallas_call(relay_kernel, out_shape=jax.ShapeDtypeStruct((PARTS, rows,...  127 us

profile of v3, /device:TPU:4, one launch (start us, length us, event | category | flops | bytes accessed | tf_op | source)
XLA Modules:
  0.0 132.9 jit_solution(2642780128310264502)
XLA Ops:
  0.0 1.4 %copy.12 = s32[1,4,4,2]{3,2,1,0:T(4,128)} copy(s32[1,4,4,2]{2,3,1,0:T(2,128)} %param.14) | data formatting | bytes 256 | tf_op jit(solution)/shard_map/reshape | solution.py:363
  1.4 1.3 %reshape.20.stop_ref = s32[2,8,1]{2,1,0:T(8,128)} reshape(s32[4,4]{1,0:T(4,128)} %param.15) | data formatting | bytes 128 | tf_op jit(solution)/shard_map/reshape | solution.py:364
  2.7 1.7 %reshape.15.x_ref = bf16[2,8,7168]{2,1,0:T(8,128)(2,1)} reshape(bf16[4,4,7168]{2,1,0:T(4,128)(2,1)} %param.8) | data formatting | bytes 458752 | tf_op jit(solution)/shard_map/reshape | solution.py:360
  4.4 126.7 %shard_map.82 = bf16[2,8,7168]{2,1,0:T(8,128)(2,1)} custom-call(bf16[2,8,7168]{2,1,0:T(8,128)(2,1)} %reshape.15.x_ref, bf16[1,7168]{1,0:T(2,128)(2,1)} %gain_ref.1, bf16[4,7168]{1,0:T(4,128)(2,1)} %bitcast.10, s32[2,8,2]{2,1,0:T(8,128)} %bitcast.11, s32[2,8,1]{2,1,0:T(8,128)} %reshape.20.stop_ref, bf16[2,7168,256]{2,1,0:T(8,128)(2,1)} %bitcast.7, ...), custom_call_target="tpu_custom_call" | custom-call | tf_op jit(solution)/shard_map/pallas_call | solution.py:329
  131.2 1.7 %reshape.19 = bf16[1,4,4,7168]{3,2,1,0:T(4,128)(2,1)} reshape(bf16[2,8,7168]{2,1,0:T(8,128)(2,1)} %shard_map.82) | data formatting | bytes 458752 | tf_op jit(solution)/shard_map/reshape | solution.py:369
